TPU v7x, 256 devices: a whole 4x4x8 slice. The times are simulated.
256 devices in a mesh: seq: 32 (over z, y), head: 8 (over x, core).
Axes of the slice: x: 4, y: 4, z: 8, core: 2. Of those that a mesh axis runs over, the one named last changes fastest.
Arguments:
- inputs: bfloat16 [32768, 5120], P('seq', 'head'), may hold values from -0.59765625 to 0.59765625
- gates: bfloat16 [32768, 5120], P('seq', 'head'), may hold values from -6 to 6
- write_keys: bfloat16 [32768, 128], P('seq'), may hold values from -6 to 6
- read_keys: bfloat16 [32768, 128], P('seq'), may hold values from -0.125 to 0.125
- log_decay: float32 [80, 32768], P('head', 'seq'), may hold values from -3 to 0
- skip_gain: float32 [80], P('head'), may hold values from 0.5 to 4
- doc_ids: int32 [32768], P('seq'), may hold values from 0 to 3, never falling along the last dimension, each value on 1 to 16384 neighbouring positions
- out_weight: bfloat16 [5120, 2560], P('head'), may hold values from -0.078125 to 0.078125
- grad_out: bfloat16 [32768, 2560], P(('seq', 'head')), may hold values from -6 to 6
Outputs:
- mixed_out: bfloat16 [32768, 2560], P(('seq', 'head'))
- grad_inputs: bfloat16 [32768, 5120], P('seq', 'head')
Inputs may be any that keep to these rules, and one draw needn't show every extreme that they name: `doc_ids`: document ids never fall along the sequence; every document has 1 to 16384 tokens and one has exactly 16384.
All inputs are finite; a program needn't handle non-finite values.
Results may differ from a plain program's by a relative error of at most 0.02.
Values may be sent and summed in bfloat16 or wider, within the bound.
A program may use at most 128 MiB of HBM per device.

v0:
```python
import jax
import jax.numpy as jnp
from jax import lax
from jax.sharding import Mesh
from jax.sharding import PartitionSpec as P

GROUP = 256
SEQ = ("seq_0", "seq_1")
HEAD = ("head_0", "head_1")
SEQ_HEAD = ("seq_0", "seq_1", "head_0", "head_1")


def passed_along(block, axis, distance):
    devices = range(lax.axis_size(axis))
    route = [(i - distance, i) for i in devices if i - distance in devices]
    return lax.ppermute(block, axis, route)


def joined_along(pieces, dim):
    pieces = jnp.moveaxis(pieces, 0, dim)
    shape = pieces.shape
    return pieces.reshape(*shape[:dim], shape[dim] * shape[dim + 1], *shape[dim + 2 :])


def gather_in_order(shard, axes, sequence):
    pieces = shard[None]
    for k in sequence:
        pieces = lax.all_gather(pieces, axes[k], axis=0, tiled=True)
    current = [lax.axis_size(axes[k]) for k in reversed(sequence)]
    pieces = pieces.reshape(*current, *shard.shape)
    turned = sorted(range(len(sequence)), key=lambda place: sequence[len(sequence) - 1 - place])
    return pieces.transpose(*turned, *range(len(sequence), pieces.ndim)).reshape(-1, *shard.shape)


def whole_of(shard, axes, sequence, dim):
    return joined_along(gather_in_order(shard, axes, sequence), dim)


def nothing_yet(shard, identity):
    return jax.tree.map(
        lambda part, zero: jnp.zeros_like(part) + jnp.asarray(zero, part.dtype), shard, identity
    )


def entering_2(shard, axes, combine, identity, reverse):
    before = start = nothing_yet(shard, identity)
    so_far = shard
    for axis in reversed(axes):
        devices, place = (lax.axis_size(axis), lax.axis_index(axis))
        pieces = jax.tree.map(
            lambda part, kind: lax.all_gather(part.astype(kind), axis),
            so_far,
            (jnp.bfloat16, jnp.bfloat16),
        )
        inside, so_far = (start, start)
        for k in reversed(range(devices)) if reverse else range(devices):
            passed = k > place if reverse else k < place
            so_far = combine(
                so_far, jax.tree.map(lambda part, own: part[k].astype(own.dtype), pieces, shard)
            )
            inside = jax.tree.map(lambda new, old: jnp.where(passed, new, old), so_far, inside)
        before = combine(inside, before)
    return before


def group_terms(write_blk, read_blk, decay_blk, doc_blk, before):
    block_len = doc_blk.shape[0]
    cumul = jnp.cumsum(decay_blk, axis=1)
    positions = jnp.arange(block_len)
    causal_same = (doc_blk[:, None] == doc_blk[None, :]) & (
        positions[:, None] >= positions[None, :]
    )
    spread = jnp.where(causal_same[None], cumul[:, :, None] - cumul[:, None, :], 0.0)
    decay_matrix = jnp.where(causal_same[None], jnp.exp(spread), 0.0)
    scores = jnp.dot(read_blk, write_blk.T, preferred_element_type=jnp.float32)
    weights = (decay_matrix * scores[None]).astype(jnp.bfloat16)
    entry_w = jnp.where((doc_blk == before)[None], jnp.exp(cumul), 0.0)
    exit_w = jnp.where(
        (doc_blk == doc_blk[block_len - 1])[None], jnp.exp(cumul[:, block_len - 1 :] - cumul), 0.0
    )
    return (weights, entry_w, exit_w, entry_w[:, block_len - 1])


def combine(earlier, later):
    return (earlier[0] * later[0], later[0][:, None, None] * earlier[1] + later[1])


def shards(
    inputs, gates, write_keys, read_keys, log_decay, skip_gain, doc_ids, out_weight, grad_out
):
    tok_rows, inner = inputs.shape
    head_count = log_decay.shape[0]
    head_width = inner // head_count
    state_width = write_keys.shape[1]
    group_count = tok_rows // GROUP
    before = passed_along(doc_ids[tok_rows - 1 :] + 1, SEQ, 1) - 1
    doc_blocks = doc_ids.reshape(group_count, GROUP)
    befores = jnp.concatenate([before, doc_blocks[:-1, GROUP - 1]])
    blocks_b = write_keys.reshape(group_count, GROUP, state_width)
    blocks_c = read_keys.reshape(group_count, GROUP, state_width)
    blocks_d = log_decay.reshape(head_count, group_count, GROUP).transpose(1, 0, 2)
    blocks_x = inputs.reshape(group_count, GROUP, head_count, head_width)
    weights, entry_w, exit_w, decays = jax.vmap(group_terms)(
        blocks_b, blocks_c, blocks_d, doc_blocks, befores
    )
    entry_t = jnp.swapaxes(entry_w, 1, 2)[..., None]
    exit_t = jnp.swapaxes(exit_w, 1, 2)[..., None]
    skip_full = skip_gain[:, None]
    inner_mixed = jnp.einsum(
        "khts,kshp->kthp", weights, blocks_x, preferred_element_type=jnp.float32
    )
    write_scaled = (exit_t * blocks_x.astype(jnp.float32)).astype(jnp.bfloat16)
    own_states = jnp.einsum(
        "kshp,ksn->khpn", write_scaled, blocks_b, preferred_element_type=jnp.float32
    )
    empty_state = jnp.zeros((head_count, head_width, state_width), jnp.float32)
    unit_decay = jnp.ones((head_count,), jnp.float32)
    running = empty_state
    run_decay = unit_decay
    enter_states = []
    enter_decays = []
    for position in range(group_count):
        enter_states.append(running)
        enter_decays.append(run_decay)
        running = decays[position][:, None, None] * running + own_states[position]
        run_decay = decays[position] * run_decay
    silu_gate = jax.nn.silu(gates.astype(jnp.float32))
    grad_gated = lax.dot_general(
        whole_of(grad_out, HEAD, (0, 1), 0),
        out_weight,
        (((1,), (1,)), ((), ())),
        preferred_element_type=jnp.float32,
    )
    grad_mix = (grad_gated * silu_gate).astype(jnp.bfloat16)
    blocks_dy = grad_mix.reshape(group_count, GROUP, head_count, head_width)
    inner_grad = jnp.einsum(
        "khts,kthp->kshp", weights, blocks_dy, preferred_element_type=jnp.float32
    )
    grad_scaled = (entry_t * blocks_dy.astype(jnp.float32)).astype(jnp.bfloat16)
    grad_states = jnp.einsum(
        "kthp,ktn->khpn", grad_scaled, blocks_c, preferred_element_type=jnp.float32
    )
    running_back = empty_state
    back_decay = unit_decay
    exit_states = []
    exit_decays = []
    for position in reversed(range(group_count)):
        exit_states.insert(0, running_back)
        exit_decays.insert(0, back_decay)
        running_back = grad_states[position] + decays[position][:, None, None] * running_back
        back_decay = decays[position] * back_decay
    state_in = entering_2((run_decay, running), SEQ, combine, (unit_decay, empty_state), False)[1]
    grad_in = entering_2((run_decay, running_back), SEQ, combine, (unit_decay, empty_state), True)[
        1
    ]
    entering = jnp.stack(
        [
            enter_states[position] + enter_decays[position][:, None, None] * state_in
            for position in range(group_count)
        ]
    ).astype(jnp.bfloat16)
    carried = (
        jnp.einsum("ktn,khpn->kthp", blocks_c, entering, preferred_element_type=jnp.float32)
        * entry_t
    )
    mixed = inner_mixed + carried + skip_full * blocks_x.astype(jnp.float32)
    gated = (mixed.reshape(tok_rows, inner) * silu_gate).astype(jnp.bfloat16)
    mixed_out = lax.psum_scatter(
        jnp.dot(gated, out_weight, preferred_element_type=jnp.float32).astype(jnp.bfloat16),
        HEAD,
        scatter_dimension=0,
        tiled=True,
    )
    arriving = jnp.stack(
        [
            exit_states[position] + exit_decays[position][:, None, None] * grad_in
            for position in range(group_count)
        ]
    ).astype(jnp.bfloat16)
    carried_grad = (
        jnp.einsum("ksn,khpn->kshp", blocks_b, arriving, preferred_element_type=jnp.float32)
        * exit_t
    )
    grad_inputs = (inner_grad + carried_grad + skip_full * blocks_dy.astype(jnp.float32)).astype(
        jnp.bfloat16
    )
    return (mixed_out, grad_inputs.reshape(tok_rows, inner))


def solution(mesh):
    split = Mesh(mesh.devices.reshape(8, 4, 4, 2), ("seq_0", "seq_1", "head_0", "head_1"))
    return jax.shard_map(
        shards,
        mesh=split,
        in_specs=(
            P(SEQ, HEAD),
            P(SEQ, HEAD),
            P(SEQ, None),
            P(SEQ, None),
            P(HEAD, SEQ),
            P(HEAD),
            P(SEQ),
            P(HEAD, None),
            P(SEQ_HEAD, None),
        ),
        out_specs=(P(SEQ_HEAD, None), P(SEQ, HEAD)),
        check_vma=False,
    )
```

profile of v0, /device:TPU:16, one launch (start us, length us, event | category | flops | bytes accessed | tf_op | source)
XLA Modules:
  0.0 246.8 jit_solution(7034171664779118965)
XLA Ops:
  8.0 1.5 slice.212
  10.1 4.5 %collective-permute-start = (s32[1]{0:T(128)}, s32[1]{0:T(128)}, u32[]{:S(2)}, u32[]{:S(2)}) collective-permute-start(s32[1]{0:T(128)} %add.280), channel_id=1, source_target_pairs={{0,8},{8,16},{16,24},{24,32},{32,40},{40,48},{48,56},{56,64},{64,7... | collective-permute-start | bytes 20 | tf_op jit(solution)/shard_map/ppermute | solution.py:16
  16.2 2.3 reduce-window.6
  19.6 2.5 %copy.66 = bf16[1024,640]{0,1:T(8,128)(2,1)} copy(bf16[1024,640]{1,0:T(8,128)(2,1)} %param.9) | data formatting | bytes 2621440 | tf_op args[0]
  23.2 1.5 exponential_select_fusion
  25.5 3.8 %reshape.401 = bf16[4,256,10,64]{1,0,3,2:T(4,128)(2,1)} reshape(bf16[1024,640]{0,1:T(8,128)(2,1)} %copy.66) | data formatting | bytes 2621440 | tf_op jit(solution)/shard_map/reshape | solution.py:102
  29.3 8.0 %all-gather = bf16[4,10,1]{1,2,0:T(2,128)(2,1)S(1)} all-gather(bf16[1,10,1]{1,2,0:T(2,128)(2,1)S(1)} %copy.68), channel_id=2, replica_groups=mesh['seq_0'=8,'seq_1'=4,'head_0'=4,'head_1'=2] {'seq_1'}, dimensions={0}, use_global_device_ids=true | all-gather | bytes 100 | tf_op jit(solution)/shard_map/all_gather | solution.py:51
  41.1 1.8 fusion.14
  44.1 13.8 %all_gather.38 = bf16[4,10,64,128]{3,2,1,0:T(8,128)(2,1)S(1)} all-gather(bf16[1,10,64,128]{3,2,1,0:T(8,128)(2,1)S(1)} %get-tuple-element.22), channel_id=1, replica_groups=mesh['seq_0'=8,'seq_1'=4,'head_0'=4,'head_1'=2] {'seq_1'}, dimensions={0}, use_global_device_ids=true | all-gather | bytes 819200 | tf_op jit(solution)/shard_map/all_gather | solution.py:51
  60.5 1.4 copy.64
  62.5 2.2 fusion.78
  66.7 17.7 %all-gather.2 = bf16[8,1,10]{2,1,0:T(2,128)(2,1)S(1)} all-gather(bf16[1,1,10]{2,1,0:T(2,128)(2,1)S(1)} %get-tuple-element.53), channel_id=1, replica_groups=mesh['seq_0'=8,'seq_1'=4,'head_0'=4,'head_1'=2] {'seq_0'}, dimensions={0}, use_global_device_ids=true | all-gather | bytes 180 | tf_op jit(solution)/shard_map/all_gather | solution.py:51
  85.5 15.2 %all-gather.9.cloned.1.call-done = bf16[8,10,64,128]{3,2,1,0:T(8,128)(2,1)} async-done(((bf16[1,10,64,128]{3,2,1,0:T(8,128)(2,1)}), bf16[8,10,64,128]{3,2,1,0:T(8,128)(2,1)}) %all-gather.9.cloned.1.call-update) | async-done | bytes 1310736 | tf_op jit(solution)/shard_map/all_gather | solution.py:51
  100.8 3.4 %fusion.76 = (bf16[1,10,64,128]{3,2,1,0:T(8,128)(2,1)}, f32[1,10,64,128]{3,2,1,0:T(8,128)}) fusion(pred[]{:T(512)S(6)} %gt.39, pred[]{:T(512)S(6)} %gt.38, pred[]{:T(512)S(6)} %gt.37, bf16[4,10,64,128]{3,2,1,0:T(8,128)(2,1)} %copy-done.2, f32[10]{0:T(128)} %copy-done.38, f32[10]{0:T(128)} %copy-done.25, f32[10]{0:T(128)S(1)} %get-tuple-element.55, ...), kind=kLoop, calls=%fused_computation.162 | loop fusion | flops 4014080 | bytes 2458132 | tf_op jit(solution)/shard_map/convert.22
  104.2 17.5 %all-gather.11.cloned.1.call-done = bf16[8,128,2560]{2,1,0:T(8,128)(2,1)} async-done(((bf16[4,128,2560]{2,1,0:T(8,128)(2,1)}), bf16[8,128,2560]{2,1,0:T(8,128)(2,1)}) %all-gather.11.cloned.1.call-update) | async-done | bytes 5242896 | tf_op jit(solution)/shard_map/all_gather | solution.py:28
  121.7 3.1 %copy.76 = bf16[4,2,128,2560]{3,2,1,0:T(8,128)(2,1)S(1)} copy(bf16[4,2,128,2560]{3,2,0,1:T(8,128)(2,1)} %bitcast.206) | data formatting | bytes 10485760 | tf_op jit(solution)/shard_map/transpose | solution.py:32
  124.9 5.4 %multiply_convert_fusion.3 = bf16[1024,640]{1,0:T(8,128)(2,1)} fusion(bf16[1024,2560]{1,0:T(8,128)(2,1)S(1)} %bitcast.207, bf16[640,2560]{1,0:T(8,128)(2,1)S(1)} %copy-done, bf16[1024,640]{1,0:T(8,128)(2,1)S(1)} %copy-done.42), kind=kOutput, calls=%fused_computation.22 | convolution fusion | flops 3360030720 | bytes 11141120 | tf_op jit(solution)/shard_map/dot_general | solution.py:128
  130.3 2.5 %copy.77 = bf16[1024,640]{0,1:T(8,128)(2,1)} copy(bf16[1024,640]{1,0:T(8,128)(2,1)} %multiply_convert_fusion.3) | data formatting | bytes 2621440 | tf_op jit(solution)/shard_map/convert_element_type | solution.py:134
  132.8 3.8 %reshape.404 = bf16[4,256,10,64]{1,0,3,2:T(4,128)(2,1)} reshape(bf16[1024,640]{0,1:T(8,128)(2,1)} %copy.77) | data formatting | bytes 2621440 | tf_op jit(solution)/shard_map/reshape | solution.py:135
  136.7 2.0 fusion.12
  140.0 12.0 %all_gather.43 = bf16[4,10,64,128]{3,2,1,0:T(8,128)(2,1)S(1)} all-gather(bf16[1,10,64,128]{3,2,1,0:T(8,128)(2,1)S(1)} %get-tuple-element.58), channel_id=1, replica_groups=mesh['seq_0'=8,'seq_1'=4,'head_0'=4,'head_1'=2] {'seq_1'}, dimensions={0}, use_global_device_ids=true | all-gather | bytes 819200 | tf_op jit(solution)/shard_map/all_gather | solution.py:51
  155.4 1.8 fusion.22
  157.2 4.1 %fusion.3 = f32[4,256,10,64]{1,3,2,0:T(8,128)S(1)} fusion(f32[4,10,64,256]{3,2,1,0:T(8,128)S(1)} %fusion.22, f32[4,256,256]{2,1,0:T(8,128)S(1)} %copy-done.11, f32[4,10,256]{2,1,0:T(8,128)S(1)} %copy-done.22, pred[4,256,256]{2,1,0:T(8,128)(4,1)S(1)} %compare_and_fusion, f32[10]{0:T(128)} %param.14, f32[4,256,10]{1,2,0:T(8,128)S(1)} %copy-done.24, ...), kind=kOutput, calls=%fused_computation.11 | convolution fusion | flops 351928320 | bytes 7946280 | tf_op jit(solution)/shard_map/khts,kshp->kthp/dot_general | solution.py:109
  161.3 1.7 copy.74
  163.0 2.1 copy.84
  165.1 3.3 %copy.75 = f32[1024,640]{1,0:T(8,128)} copy(f32[1024,640]{0,1:T(8,128)} %bitcast.205) | data formatting | bytes 5242880 | tf_op jit(solution)/shard_map/reshape | solution.py:167
  168.3 8.8 %convolution_convert_fusion = bf16[1024,2560]{1,0:T(8,128)(2,1)} fusion(bf16[640,2560]{1,0:T(8,128)(2,1)S(1)} %copy-done, f32[1024,640]{1,0:T(8,128)} %copy.75, bf16[1024,640]{1,0:T(8,128)(2,1)} %param.10), kind=kOutput, calls=%fused_computation.1 | convolution fusion | flops 3362652160 | bytes 12451840 | tf_op jit(solution)/shard_map/dot_general | solution.py:169
  177.2 17.2 %all-gather.3 = bf16[8,1,10]{2,1,0:T(2,128)(2,1)S(1)} all-gather(bf16[1,1,10]{2,1,0:T(2,128)(2,1)} %get-tuple-element.52), channel_id=1, replica_groups=mesh['seq_0'=8,'seq_1'=4,'head_0'=4,'head_1'=2] {'seq_0'}, dimensions={0}, use_global_device_ids=true | all-gather | bytes 180 | tf_op jit(solution)/shard_map/all_gather | solution.py:51
  196.1 2.7 %add_convert_fusion.2 = (bf16[1,10,64,128]{3,2,1,0:T(8,128)(2,1)S(1)}, f32[1,10,64,128]{3,2,1,0:T(8,128)S(1)}) fusion(f32[10]{0:T(128)} %get-tuple-element.14, f32[1,10,64,128]{3,2,1,0:T(8,128)} %get-tuple-element.59, f32[10]{0:T(128)S(1)} %get-tuple-element.10, f32[4,10,64,128]{3,2,1,0:T(8,128)} %copy-done.3, pred[]{:T(512)S(6)} %lt.39, pred[]{:T(512)S(6)} %lt.38, ...), kind=kLoop, calls=%fused_computation.61 | loop fusion | flops 4341760 | bytes 3113572 | tf_op jit(solution)/shard_map/convert.18
  200.8 3.6 %fusion.9 = bf16[4,256,10,64]{1,3,2,0:T(8,128)(2,1)S(1)} fusion(f32[4,10,64,256]{3,2,1,0:T(8,128)S(1)} %fusion.30, f32[4,256,256]{2,1,0:T(8,128)S(1)} %copy-done.12, f32[4,10,256]{2,1,0:T(8,128)S(1)} %copy-done.23, pred[4,256,256]{2,1,0:T(8,128)(4,1)S(1)} %copy-done.19, f32[10]{0:T(128)S(1)} %copy-done.43, f32[4,256,10]{1,2,0:T(8,128)S(1)} %copy-done.21, ...), kind=kOutput, calls=%fused_computation.17 | convolution fusion | flops 352583680 | bytes 6635560 | tf_op jit(solution)/shard_map/khts,kthp->kshp/dot_general | solution.py:136
  206.8 2.4 copy.81
  209.2 31.0 %reduce-scatter.2.cloned.1.call-done = bf16[128,2560]{1,0:T(8,128)(2,1)} async-done(((bf16[1024,2560]{1,0:T(8,128)(2,1)}), bf16[128,2560]{1,0:T(8,128)(2,1)}) %reduce-scatter.2.cloned.1.call-update) | async-done | bytes 655376 | tf_op jit(solution)/shard_map/reduce_scatter | solution.py:168
  (143 shorter events, 26.5 us)
Async XLA Ops:
  7.2 117.7 %copy-start = (bf16[640,2560]{1,0:T(8,128)(2,1)S(1)}, bf16[640,2560]{1,0:T(8,128)(2,1)}, u32[]{:S(2)}) copy-start(bf16[640,2560]{1,0:T(8,128)(2,1)} %param.16) | copy-start | bytes 9830404
  7.2 52.6 %all-gather.15.cloned.1.call-start = ((), (), s32[]{:S(2)}) async-start(), calls=%async_computation.5 | async-start | bytes 3276800 | tf_op jit(solution)/shard_map/all_gather | solution.py:28
  7.9 92.9 %all-gather.9.cloned.1.call-start = ((), (), s32[]{:S(2)}) async-start(), calls=%async_computation.1 | async-start | bytes 1474560 | tf_op jit(solution)/shard_map/all_gather | solution.py:51
  10.1 12.3 %collective-permute-start = (s32[1]{0:T(128)}, s32[1]{0:T(128)}, u32[]{:S(2)}, u32[]{:S(2)}) collective-permute-start(s32[1]{0:T(128)} %add.280), channel_id=1, source_target_pairs={{0,8},{8,16},{16,24},{24,32},{32,40},{40,48},{48,56},{56,64},{64,7... | collective-permute-start | bytes 20 | tf_op jit(solution)/shard_map/ppermute | solution.py:16
  19.6 21.5 %copy-start.14 = (bf16[1024,128]{1,0:T(8,128)(2,1)S(1)}, bf16[1024,128]{1,0:T(8,128)(2,1)}, u32[]{:S(2)}) copy-start(bf16[1024,128]{1,0:T(8,128)(2,1)} %param.11) | copy-start | bytes 786436
  38.1 19.8 %copy-start.20 = (f32[4,256,10]{1,2,0:T(8,128)}, f32[4,256,10]{1,2,0:T(8,128)S(1)}, u32[]{:S(2)}) copy-start(f32[4,256,10]{1,2,0:T(8,128)S(1)} %copy.71) | copy-start | bytes 122884
  39.2 18.6 %copy-start.27 = (f32[10]{0:T(128)}, f32[10]{0:T(128)S(1)}, u32[]{:S(2)}) copy-start(f32[10]{0:T(128)S(1)} %get-tuple-element.11) | copy-start | bytes 124
  39.3 18.6 %copy-start.29 = (f32[10]{0:T(128)}, f32[10]{0:T(128)S(1)}, u32[]{:S(2)}) copy-start(f32[10]{0:T(128)S(1)} %get-tuple-element.8) | copy-start | bytes 124
  39.8 18.0 %copy-start.25 = (f32[10]{0:T(128)}, f32[10]{0:T(128)S(1)}, u32[]{:S(2)}) copy-start(f32[10]{0:T(128)S(1)} %get-tuple-element.56) | copy-start | bytes 124
  39.8 18.0 %copy-start.39 = (f32[10]{0:T(128)}, f32[10]{0:T(128)S(1)}, u32[]{:S(2)}) copy-start(f32[10]{0:T(128)S(1)} %get-tuple-element.57) | copy-start | bytes 124
  40.4 17.4 %copy-start.38 = (f32[10]{0:T(128)}, f32[10]{0:T(128)S(1)}, u32[]{:S(2)}) copy-start(f32[10]{0:T(128)S(1)} %get-tuple-element.49) | copy-start | bytes 124
  41.1 16.8 %copy-start.33 = (f32[10]{0:T(128)}, f32[10]{0:T(128)S(1)}, u32[]{:S(2)}) copy-start(f32[10]{0:T(128)S(1)} %get-tuple-element.62) | copy-start | bytes 124
  44.1 18.4 %copy-start.13 = (bf16[1024,128]{1,0:T(8,128)(2,1)S(1)}, bf16[1024,128]{1,0:T(8,128)(2,1)}, u32[]{:S(2)}) copy-start(bf16[1024,128]{1,0:T(8,128)(2,1)} %param.12) | copy-start | bytes 786436
  59.7 62.0 %all-gather.11.cloned.1.call-start = ((), (), s32[]{:S(2)}) async-start(), calls=%async_computation.3 | async-start | bytes 7864320 | tf_op jit(solution)/shard_map/all_gather | solution.py:28
  60.4 135.7 %all-gather.13.cloned.1.call-start = ((), (), s32[]{:S(2)}) async-start(), calls=%async_computation.4 | async-start | bytes 1474560 | tf_op jit(solution)/shard_map/all_gather | solution.py:51
  121.7 3.2 %copy-start.42 = (bf16[1024,640]{1,0:T(8,128)(2,1)S(1)}, bf16[1024,640]{1,0:T(8,128)(2,1)}, u32[]{:S(2)}) copy-start(bf16[1024,640]{1,0:T(8,128)(2,1)} %param.10) | copy-start | bytes 3932164
  136.6 2.1 copy-start.31
  136.6 2.1 copy-start.34
  136.6 2.1 copy-start.37
  136.6 2.1 copy-start.40
  138.7 14.2 %copy-start.26 = (f32[10]{0:T(128)S(1)}, f32[10]{0:T(128)}, u32[]{:S(2)}) copy-start(f32[10]{0:T(128)} %copy-done.25) | copy-start | bytes 124
  138.7 14.2 %copy-start.32 = (f32[10]{0:T(128)S(1)}, f32[10]{0:T(128)}, u32[]{:S(2)}) copy-start(f32[10]{0:T(128)} %get-tuple-element.50) | copy-start | bytes 124
  138.7 14.2 %copy-start.35 = (f32[10]{0:T(128)S(1)}, f32[10]{0:T(128)}, u32[]{:S(2)}) copy-start(f32[10]{0:T(128)} %get-tuple-element.54) | copy-start | bytes 124
  153.8 86.4 %reduce-scatter.2.cloned.1.call-start = ((), (), s32[]{:S(2)}) async-start(), calls=%async_computation.2 | async-start | bytes 5898240 | tf_op jit(solution)/shard_map/reduce_scatter | solution.py:168
  154.1 3.1 %copy-start.7 = (bf16[4,256,10,64]{1,0,3,2:T(4,128)(2,1)S(1)}, bf16[4,256,10,64]{1,0,3,2:T(4,128)(2,1)}, u32[]{:S(2)}) copy-start(bf16[4,256,10,64]{1,0,3,2:T(4,128)(2,1)} %reshape.401) | copy-start | bytes 3932164
  154.1 3.1 %copy-start.11 = (f32[4,256,256]{2,1,0:T(8,128)S(1)}, f32[4,256,256]{2,1,0:T(8,128)}, u32[]{:S(2)}) copy-start(f32[4,256,256]{2,1,0:T(8,128)} %fusion.78) | copy-start | bytes 3145732
  154.1 3.1 %copy-start.22 = (f32[4,10,256]{2,1,0:T(8,128)S(1)}, f32[4,10,256]{2,1,0:T(8,128)}, u32[]{:S(2)}) copy-start(f32[4,10,256]{2,1,0:T(8,128)} %copy.64) | copy-start | bytes 122884
  154.1 3.1 %copy-start.24 = (f32[4,256,10]{1,2,0:T(8,128)S(1)}, f32[4,256,10]{1,2,0:T(8,128)}, u32[]{:S(2)}) copy-start(f32[4,256,10]{1,2,0:T(8,128)} %copy.73) | copy-start | bytes 122884
  155.4 5.9 %copy-start.18 = (pred[4,256,256]{2,1,0:T(8,128)(4,1)}, pred[4,256,256]{2,1,0:T(8,128)(4,1)S(1)}, u32[]{:S(2)}) copy-start(pred[4,256,256]{2,1,0:T(8,128)(4,1)S(1)} %compare_and_fusion) | copy-start | bytes 786436
  177.1 21.7 %copy-start.28 = (f32[10]{0:T(128)S(1)}, f32[10]{0:T(128)}, u32[]{:S(2)}) copy-start(f32[10]{0:T(128)} %copy-done.27) | copy-start | bytes 124
  177.2 23.0 %copy-start.15 = (bf16[1024,128]{1,0:T(8,128)(2,1)S(1)}, bf16[1024,128]{1,0:T(8,128)(2,1)}, u32[]{:S(2)}) copy-start(bf16[1024,128]{1,0:T(8,128)(2,1)} %param.11) | copy-start | bytes 786436
  196.1 2.8 %copy-start.6 = (f32[1,10,64,128]{3,2,1,0:T(8,128)S(1)}, f32[1,10,64,128]{3,2,1,0:T(8,128)}, u32[]{:S(2)}) copy-start(f32[1,10,64,128]{3,2,1,0:T(8,128)} %get-tuple-element.59) | copy-start | bytes 983044
  (18 other events, 29.3 us)
Sparse Core Ops, SparseCore 0:
  9.8 40.5 all-gather.14
  59.8 40.9 all-gather.8
  102.6 19.0 all-gather.10
  154.0 42.0 all-gather.12
  199.0 41.1 reduce-scatter.1
where the time goes:
time: 248 us; the launch traced here: 247 us
  blocking collectives  68.6 us (28%)
  waiting for transfers between devices  65.7 us (26%)
  local copies, waits for them, and re-layouts  39.3 us (16%)
  matrix products  30.2 us (12%)
  other arithmetic  22.3 us (9%)
  between operations  15.8 us (6%)
  starting transfers between devices  4.85 us (2%)
    all_gather x5, blocking collectives, entering_2(): lax.all_gather(part.astype(kind), axis)  68.6 us
    reduce_scatter x1, waiting for transfers between devices, shards(): lax.psum_scatter(jnp.dot(gated, out_weight, preferred_element_type=jnp.fl...  31 us
    all_gather x2, waiting for transfers between devices, gather_in_order(): pieces = lax.all_gather(pieces, axes[k], axis=0, tiled=True)  17.5 us
    all_gather x2, waiting for transfers between devices, entering_2(): lax.all_gather(part.astype(kind), axis)  15.8 us
    unnamed x92, local copies, waits for them, and re-layouts  11.3 us
    another operation x7, other arithmetic  11.1 us
    dot_general x1, matrix products, shards(): jnp.dot(gated, out_weight, preferred_element_type=jnp.float32)  8.8 us
    dot_general x1, matrix products, shards(): lax.dot_general(whole_of(grad_out, HEAD, (0, 1), 0), out_weight, (((1,),...  5.44 us
  transfers between devices with their start and end apart: 6, of which 4 were waited for; matrix products, arithmetic and copies ran while one was open for 28% of the time, Pallas kernels for 0%

commit v1 on v0

--- a/solution.py
+++ b/solution.py
@@ -25,7 +25,10 @@
 def gather_in_order(shard, axes, sequence):
     pieces = shard[None]
     for k in sequence:
-        pieces = lax.all_gather(pieces, axes[k], axis=0, tiled=True)
+        size = lax.axis_size(axes[k])
+        parts = jnp.stack([pieces for _ in range(size)])
+        parts = lax.all_to_all(parts, axes[k], split_axis=0, concat_axis=0)
+        pieces = jnp.concatenate(parts, axis=0)
     current = [lax.axis_size(axes[k]) for k in reversed(sequence)]
     pieces = pieces.reshape(*current, *shard.shape)
     turned = sorted(range(len(sequence)), key=lambda place: sequence[len(sequence) - 1 - place])

time: 248 us -> 230 us (0.927)
  waiting for transfers between devices: 65.7 us -> 32 us
  blocking collectives: 68.6 us -> 75.1 us
  starting transfers between devices: 4.85 us -> 9.47 us
  other arithmetic: 22.3 us -> 26.9 us
    all_gather x2 -> x0, waiting for transfers between devices: 17.5 us -> none  [gather_in_order(): pieces = lax.all_gather(pieces, axes[k], axis=0, tiled=True)]
    all_gather x2, waiting for transfers between devices: 15.8 us -> 0.74 us  [entering_2(): lax.all_gather(part.astype(kind), axis)]
    all_to_all x0 -> x1, blocking collectives: none -> 7.95 us  [gather_in_order(): parts = lax.all_to_all(parts, axes[k], split_axis=0, concat_axis=0)]
    all_to_all x0 -> x1, starting transfers between devices: none -> 4.69 us  [gather_in_order(): parts = lax.all_to_all(parts, axes[k], split_axis=0, concat_axis=0)]
    another operation x7 -> x8, other arithmetic: 11.1 us -> 15 us
    transpose x1 -> x0, local copies, waits for them, and re-layouts: 3.14 us -> none  [gather_in_order(): pieces.transpose(*turned, *range(len(sequence), pieces.ndim))]
    unnamed x92 -> x78, local copies, waits for them, and re-layouts: 11.3 us -> 11.8 us
  transfers between devices with their start and end apart: 6 -> 5, of which waited for: 4 -> 2; matrix products, arithmetic and copies ran while one was open for 28% -> 37% of each run, Pallas kernels for 0% -> 0%
where the time goes in v1:
time: 230 us; the launch traced here: 228 us
  blocking collectives  75.1 us (33%)
  local copies, waits for them, and re-layouts  38 us (17%)
  waiting for transfers between devices  32 us (14%)
  matrix products  31.3 us (14%)
  other arithmetic  26.9 us (12%)
  between operations  15.6 us (7%)
  starting transfers between devices  9.47 us (4%)
    all_gather x5, blocking collectives, entering_2(): lax.all_gather(part.astype(kind), axis)  67.1 us
    reduce_scatter x1, waiting for transfers between devices, shards(): lax.psum_scatter(jnp.dot(gated, out_weight, preferred_element_type=jnp.fl...  31.2 us
    another operation x7, other arithmetic  12 us
    unnamed x78, local copies, waits for them, and re-layouts  11.8 us
    dot_general x1, matrix products, shards(): jnp.dot(gated, out_weight, preferred_element_type=jnp.float32)  8.78 us
    all_to_all x1, blocking collectives, gather_in_order(): parts = lax.all_to_all(parts, axes[k], split_axis=0, concat_axis=0)  7.95 us
    dot_general x1, matrix products, shards(): lax.dot_general(whole_of(grad_out, HEAD, (0, 1), 0), out_weight, (((1,),...  5.46 us
    all_to_all x1, starting transfers between devices, gather_in_order(): parts = lax.all_to_all(parts, axes[k], split_axis=0, concat_axis=0)  4.69 us
  transfers between devices with their start and end apart: 5, of which 2 were waited for; matrix products, arithmetic and copies ran while one was open for 37% of the time, Pallas kernels for 0%

profile of v1, /device:TPU:16, one launch (start us, length us, event | category | flops | bytes accessed | tf_op | source)
XLA Modules:
  0.0 228.4 jit_solution(16081189033949292778)
XLA Ops:
  9.3 4.5 %collective-permute-start = (s32[1]{0:T(128)}, s32[1]{0:T(128)}, u32[]{:S(2)}, u32[]{:S(2)}) collective-permute-start(s32[1]{0:T(128)} %add.280), channel_id=1, source_target_pairs={{0,8},{8,16},{16,24},{24,32},{32,40},{40,48},{48,56},{56,64},{64,7... | collective-permute-start | bytes 20 | tf_op jit(solution)/shard_map/ppermute | solution.py:16
  13.7 2.8 %stack.11 = bf16[4,1,128,2560]{3,2,1,0:T(8,128)(2,1)} broadcast(bf16[128,2560]{1,0:T(8,128)(2,1)} %param.17), dimensions={2,3} | broadcast | bytes 3276800 | tf_op jit(solution)/shard_map/stack | solution.py:29
  16.6 4.7 %all-to-all-start = ((bf16[4,1,128,2560]{3,2,1,0:T(8,128)(2,1)}), bf16[4,1,128,2560]{3,2,1,0:T(8,128)(2,1)}, u32[]{:S(2)}, u32[]{:S(2)}) async-start(bf16[4,1,128,2560]{3,2,1,0:T(8,128)(2,1)} %stack.11), calls=%async_computation.1 | async-start | bytes 5242880 | tf_op jit(solution)/shard_map/all_to_all | solution.py:30
  22.3 2.3 %reduce-window.6 = f32[4,10,2,128]{3,1,2,0:T(8,128)S(1)} reduce-window(f32[4,10,2,128]{3,1,2,0:T(8,128)S(1)} %copy.59, f32[]{:T(128)} %constant.15.clone.1), window={size=1x1x1x128 pad=0_0x0_0x0_0x127_0}, to_apply=%region_0.0 | reduce-window | flops 1300480 | bytes 81924 | tf_op jit(solution)/shard_map/reduce-window
  26.6 2.5 %copy.65 = bf16[1024,640]{0,1:T(8,128)(2,1)} copy(bf16[1024,640]{1,0:T(8,128)(2,1)} %param.9) | data formatting | bytes 2621440 | tf_op args[0]
  29.1 3.8 %reshape.400 = bf16[4,256,10,64]{1,0,3,2:T(4,128)(2,1)} reshape(bf16[1024,640]{0,1:T(8,128)(2,1)} %copy.65) | data formatting | bytes 2621440 | tf_op jit(solution)/shard_map/reshape | solution.py:105
  32.9 2.3 fusion.78
  36.5 1.5 exponential_select_fusion
  38.8 7.9 %all-gather = bf16[4,10,1]{1,2,0:T(2,128)(2,1)S(1)} all-gather(bf16[1,10,1]{1,2,0:T(2,128)(2,1)S(1)} %copy.67), channel_id=2, replica_groups=mesh['seq_0'=8,'seq_1'=4,'head_0'=4,'head_1'=2] {'seq_1'}, dimensions={0}, use_global_device_ids=true | all-gather | bytes 100 | tf_op jit(solution)/shard_map/all_gather | solution.py:54
  50.6 1.8 fusion.14
  53.6 13.6 %all_gather.32 = bf16[4,10,64,128]{3,2,1,0:T(8,128)(2,1)S(1)} all-gather(bf16[1,10,64,128]{3,2,1,0:T(8,128)(2,1)S(1)} %get-tuple-element.22), channel_id=1, replica_groups=mesh['seq_0'=8,'seq_1'=4,'head_0'=4,'head_1'=2] {'seq_1'}, dimensions={0}, use_global_device_ids=true | all-gather | bytes 819200 | tf_op jit(solution)/shard_map/all_gather | solution.py:54
  71.1 17.7 %all-gather.1 = bf16[8,1,10]{2,1,0:T(2,128)(2,1)S(1)} all-gather(bf16[1,1,10]{2,1,0:T(2,128)(2,1)S(1)} %get-tuple-element.53), channel_id=1, replica_groups=mesh['seq_0'=8,'seq_1'=4,'head_0'=4,'head_1'=2] {'seq_0'}, dimensions={0}, use_global_device_ids=true | all-gather | bytes 180 | tf_op jit(solution)/shard_map/all_gather | solution.py:54
  90.0 3.0 %pad_maximum_fusion = bf16[2,4,128,2560]{3,2,1,0:T(8,128)(2,1)S(1)} fusion(bf16[1,4,128,2560]{3,2,1,0:T(8,128)(2,1)} %bitcast.30), kind=kLoop, calls=%fused_computation.2 | loop fusion | flops 2621440 | bytes 7864320 | tf_op jit(solution)/shard_map/stack | solution.py:29
  93.0 7.9 %all_to_all.10 = bf16[2,4,128,2560]{3,2,1,0:T(8,128)(2,1)S(1)} all-to-all(bf16[2,4,128,2560]{3,2,1,0:T(8,128)(2,1)S(1)} %pad_maximum_fusion), channel_id=1, replica_groups=mesh['seq_0'=8,'seq_1'=4,'head_0'=4,'head_1'=2] {'head_1'}, dimensions={0} | all-to-all | bytes 10485760 | tf_op jit(solution)/shard_map/all_to_all | solution.py:30
  102.3 5.5 %multiply_convert_fusion.3 = bf16[1024,640]{1,0:T(8,128)(2,1)} fusion(bf16[1024,2560]{1,0:T(8,128)(2,1)S(1)} %bitcast.205, bf16[640,2560]{1,0:T(8,128)(2,1)S(1)} %copy-done, bf16[1024,640]{1,0:T(8,128)(2,1)S(1)} %copy-done.35), kind=kOutput, calls=%fused_computation.23 | convolution fusion | flops 3360030720 | bytes 11141120 | tf_op jit(solution)/shard_map/dot_general | solution.py:131
  107.7 2.5 %copy.76 = bf16[1024,640]{0,1:T(8,128)(2,1)} copy(bf16[1024,640]{1,0:T(8,128)(2,1)} %multiply_convert_fusion.3) | data formatting | bytes 2621440 | tf_op jit(solution)/shard_map/convert_element_type | solution.py:137
  110.2 3.8 %reshape.402 = bf16[4,256,10,64]{1,0,3,2:T(4,128)(2,1)} reshape(bf16[1024,640]{0,1:T(8,128)(2,1)} %copy.76) | data formatting | bytes 2621440 | tf_op jit(solution)/shard_map/reshape | solution.py:138
  114.0 3.0 %fusion.12 = f32[4,10,64,128]{3,2,1,0:T(8,128)} fusion(bf16[4,256,128,1]{2,1,3,0:T(8,128)(2,1)S(1)} %bitcast.209, f32[4,256,10]{1,2,0:T(8,128)} %copy.72, bf16[4,256,10,64]{1,0,3,2:T(4,128)(2,1)} %reshape.402), kind=kOutput, calls=%fused_computation.25 | convolution fusion | flops 169738240 | bytes 2924544 | tf_op jit(solution)/shard_map/kthp,ktn->khpn/dot_general | solution.py:143
  116.9 3.4 %fusion.76 = (bf16[1,10,64,128]{3,2,1,0:T(8,128)(2,1)}, f32[1,10,64,128]{3,2,1,0:T(8,128)S(1)}) fusion(pred[]{:T(512)S(6)} %gt.39, pred[]{:T(512)S(6)} %gt.38, pred[]{:T(512)S(6)} %gt.37, bf16[4,10,64,128]{3,2,1,0:T(8,128)(2,1)} %copy-done.2, f32[10]{0:T(128)} %copy-done.32, f32[10]{0:T(128)S(1)} %copy-done.24, f32[10]{0:T(128)S(1)} %get-tuple-element.55, ...), kind=kLoop, calls=%fused_computation.163 | loop fusion | flops 4014080 | bytes 2458132 | tf_op jit(solution)/shard_map/convert.22
  120.3 2.2 add_convert_fusion.5
  122.5 13.4 %all_gather.35 = bf16[4,10,64,128]{3,2,1,0:T(8,128)(2,1)S(1)} all-gather(bf16[1,10,64,128]{3,2,1,0:T(8,128)(2,1)S(1)} %get-tuple-element.58), channel_id=1, replica_groups=mesh['seq_0'=8,'seq_1'=4,'head_0'=4,'head_1'=2] {'seq_1'}, dimensions={0}, use_global_device_ids=true | all-gather | bytes 819200 | tf_op jit(solution)/shard_map/all_gather | solution.py:54
  139.3 1.8 fusion.22
  141.1 4.1 %fusion.3 = f32[4,256,10,64]{1,3,2,0:T(8,128)S(1)} fusion(f32[4,10,64,256]{3,2,1,0:T(8,128)S(1)} %fusion.22, f32[4,256,256]{2,1,0:T(8,128)S(1)} %copy-done.9, f32[4,10,256]{2,1,0:T(8,128)S(1)} %copy-done.18, pred[4,256,256]{2,1,0:T(8,128)(4,1)S(1)} %compare_and_fusion, f32[10]{0:T(128)} %param.14, f32[4,256,10]{1,2,0:T(8,128)S(1)} %copy-done.22, ...), kind=kOutput, calls=%fused_computation.12 | convolution fusion | flops 351928320 | bytes 7946280 | tf_op jit(solution)/shard_map/khts,kshp->kthp/dot_general | solution.py:112
  145.2 1.7 copy.73
  146.9 2.1 copy.83
  149.0 3.3 %copy.74 = f32[1024,640]{1,0:T(8,128)} copy(f32[1024,640]{0,1:T(8,128)} %bitcast.204) | data formatting | bytes 5242880 | tf_op jit(solution)/shard_map/reshape | solution.py:170
  152.2 8.8 %convolution_convert_fusion = bf16[1024,2560]{1,0:T(8,128)(2,1)} fusion(bf16[640,2560]{1,0:T(8,128)(2,1)S(1)} %copy-done, f32[1024,640]{1,0:T(8,128)} %copy.74, bf16[1024,640]{1,0:T(8,128)(2,1)} %param.10), kind=kOutput, calls=%fused_computation.1 | convolution fusion | flops 3362652160 | bytes 12451840 | tf_op jit(solution)/shard_map/dot_general | solution.py:172
  161.1 14.4 %all-gather.2 = bf16[8,1,10]{2,1,0:T(2,128)(2,1)S(1)} all-gather(bf16[1,1,10]{2,1,0:T(2,128)(2,1)} %get-tuple-element.52), channel_id=1, replica_groups=mesh['seq_0'=8,'seq_1'=4,'head_0'=4,'head_1'=2] {'seq_0'}, dimensions={0}, use_global_device_ids=true | all-gather | bytes 180 | tf_op jit(solution)/shard_map/all_gather | solution.py:54
  177.5 2.7 %add_convert_fusion.2 = (bf16[1,10,64,128]{3,2,1,0:T(8,128)(2,1)S(1)}, f32[1,10,64,128]{3,2,1,0:T(8,128)S(1)}) fusion(f32[10]{0:T(128)} %get-tuple-element.14, f32[1,10,64,128]{3,2,1,0:T(8,128)} %get-tuple-element.59, f32[10]{0:T(128)S(1)} %get-tuple-element.10, f32[4,10,64,128]{3,2,1,0:T(8,128)} %fusion.12, pred[]{:T(512)S(6)} %lt.39, pred[]{:T(512)S(6)} %lt.38, ...), kind=kLoop, calls=%fused_computation.62 | loop fusion | flops 4341760 | bytes 3113572 | tf_op jit(solution)/shard_map/convert.18
  182.2 3.6 %fusion.9 = bf16[4,256,10,64]{1,3,2,0:T(8,128)(2,1)S(1)} fusion(f32[4,10,64,256]{3,2,1,0:T(8,128)S(1)} %fusion.30, f32[4,256,256]{2,1,0:T(8,128)S(1)} %copy-done.10, f32[4,10,256]{2,1,0:T(8,128)S(1)} %copy-done.19, pred[4,256,256]{2,1,0:T(8,128)(4,1)S(1)} %copy-done.16, f32[10]{0:T(128)S(1)} %copy-done.36, f32[4,256,10]{1,2,0:T(8,128)S(1)} %copy-done.21, ...), kind=kOutput, calls=%fused_computation.18 | convolution fusion | flops 352583680 | bytes 6635560 | tf_op jit(solution)/shard_map/khts,kthp->kshp/dot_general | solution.py:139
  188.2 2.4 %copy.80 = bf16[1024,640]{1,0:T(8,128)(2,1)} copy(bf16[1024,640]{0,1:T(8,128)(2,1)} %bitcast.207) | data formatting | bytes 2621440
  190.6 31.2 %reduce-scatter.2.cloned.1.call-done = bf16[128,2560]{1,0:T(8,128)(2,1)} async-done(((bf16[1024,2560]{1,0:T(8,128)(2,1)}), bf16[128,2560]{1,0:T(8,128)(2,1)}) %reduce-scatter.2.cloned.1.call-update) | async-done | bytes 655376 | tf_op jit(solution)/shard_map/reduce_scatter | solution.py:171
  (128 shorter events, 26.6 us)
Async XLA Ops:
  7.2 94.1 %copy-start = (bf16[640,2560]{1,0:T(8,128)(2,1)S(1)}, bf16[640,2560]{1,0:T(8,128)(2,1)}, u32[]{:S(2)}) copy-start(bf16[640,2560]{1,0:T(8,128)(2,1)} %param.16) | copy-start | bytes 9830404
  9.3 25.9 %collective-permute-start = (s32[1]{0:T(128)}, s32[1]{0:T(128)}, u32[]{:S(2)}, u32[]{:S(2)}) collective-permute-start(s32[1]{0:T(128)} %add.280), channel_id=1, source_target_pairs={{0,8},{8,16},{16,24},{24,32},{32,40},{40,48},{48,56},{56,64},{64,7... | collective-permute-start | bytes 20 | tf_op jit(solution)/shard_map/ppermute | solution.py:16
  16.6 4.8 %copy-start.34 = (s32[1024]{0:T(1024)S(1)}, s32[1024]{0:T(1024)}, u32[]{:S(2)}) copy-start(s32[1024]{0:T(1024)} %param.15) | copy-start | bytes 12292
  16.6 5.7 %copy-start.17 = (f32[10,1024]{1,0:T(8,128)S(1)}, f32[10,1024]{1,0:T(8,128)}, u32[]{:S(2)}) copy-start(f32[10,1024]{1,0:T(8,128)} %param.13) | copy-start | bytes 122884
  16.6 73.4 %all-to-all-start = ((bf16[4,1,128,2560]{3,2,1,0:T(8,128)(2,1)}), bf16[4,1,128,2560]{3,2,1,0:T(8,128)(2,1)}, u32[]{:S(2)}, u32[]{:S(2)}) async-start(bf16[4,1,128,2560]{3,2,1,0:T(8,128)(2,1)} %stack.11), calls=%async_computation.1 | async-start | bytes 5242880 | tf_op jit(solution)/shard_map/all_to_all | solution.py:30
  21.3 95.7 %all-gather.6.cloned.1.call-start = ((), (), s32[]{:S(2)}) async-start(), calls=%async_computation.3 | async-start | bytes 1474560 | tf_op jit(solution)/shard_map/all_gather | solution.py:54
  26.6 6.2 %copy-start.11 = (bf16[1024,128]{1,0:T(8,128)(2,1)S(1)}, bf16[1024,128]{1,0:T(8,128)(2,1)}, u32[]{:S(2)}) copy-start(bf16[1024,128]{1,0:T(8,128)(2,1)} %param.12) | copy-start | bytes 786436
  47.3 20.0 %copy-start.23 = (f32[10]{0:T(128)}, f32[10]{0:T(128)S(1)}, u32[]{:S(2)}) copy-start(f32[10]{0:T(128)S(1)} %get-tuple-element.56) | copy-start | bytes 124
  47.3 20.0 %copy-start.33 = (f32[10]{0:T(128)}, f32[10]{0:T(128)S(1)}, u32[]{:S(2)}) copy-start(f32[10]{0:T(128)S(1)} %get-tuple-element.57) | copy-start | bytes 124
  47.9 19.4 %copy-start.32 = (f32[10]{0:T(128)}, f32[10]{0:T(128)S(1)}, u32[]{:S(2)}) copy-start(f32[10]{0:T(128)S(1)} %get-tuple-element.49) | copy-start | bytes 124
  49.1 18.1 %copy-start.25 = (f32[10]{0:T(128)}, f32[10]{0:T(128)S(1)}, u32[]{:S(2)}) copy-start(f32[10]{0:T(128)S(1)} %get-tuple-element.11) | copy-start | bytes 124
  49.1 18.1 %copy-start.27 = (f32[10]{0:T(128)}, f32[10]{0:T(128)S(1)}, u32[]{:S(2)}) copy-start(f32[10]{0:T(128)S(1)} %get-tuple-element.8) | copy-start | bytes 124
  49.9 17.3 %copy-start.20 = (f32[4,256,10]{1,2,0:T(8,128)}, f32[4,256,10]{1,2,0:T(8,128)S(1)}, u32[]{:S(2)}) copy-start(f32[4,256,10]{1,2,0:T(8,128)S(1)} %copy.70) | copy-start | bytes 122884
  50.6 16.7 %copy-start.29 = (f32[10]{0:T(128)}, f32[10]{0:T(128)S(1)}, u32[]{:S(2)}) copy-start(f32[10]{0:T(128)S(1)} %get-tuple-element.62) | copy-start | bytes 124
  69.1 108.4 %all-gather.8.cloned.1.call-start = ((), (), s32[]{:S(2)}) async-start(), calls=%async_computation.5 | async-start | bytes 1474560 | tf_op jit(solution)/shard_map/all_gather | solution.py:54
  110.2 6.7 %copy-start.24 = (f32[10]{0:T(128)S(1)}, f32[10]{0:T(128)}, u32[]{:S(2)}) copy-start(f32[10]{0:T(128)} %copy-done.23) | copy-start | bytes 124
  116.9 3.4 %copy-start.3 = (f32[4,10,64,128]{3,2,1,0:T(8,128)S(1)}, f32[4,10,64,128]{3,2,1,0:T(8,128)}, u32[]{:S(2)}) copy-start(f32[4,10,64,128]{3,2,1,0:T(8,128)} %fusion.12) | copy-start | bytes 3932164
  116.9 3.4 %copy-start.8 = (f32[1,10,64,128]{3,2,1,0:T(8,128)S(1)}, f32[1,10,64,128]{3,2,1,0:T(8,128)}, u32[]{:S(2)}) copy-start(f32[1,10,64,128]{3,2,1,0:T(8,128)} %get-tuple-element.23) | copy-start | bytes 983044
  120.3 16.5 %copy-start.28 = (f32[10]{0:T(128)S(1)}, f32[10]{0:T(128)}, u32[]{:S(2)}) copy-start(f32[10]{0:T(128)} %get-tuple-element.50) | copy-start | bytes 124
  120.3 16.5 %copy-start.30 = (f32[10]{0:T(128)S(1)}, f32[10]{0:T(128)}, u32[]{:S(2)}) copy-start(f32[10]{0:T(128)} %get-tuple-element.54) | copy-start | bytes 124
  137.8 84.1 %reduce-scatter.2.cloned.1.call-start = ((), (), s32[]{:S(2)}) async-start(), calls=%async_computation.4 | async-start | bytes 5898240 | tf_op jit(solution)/shard_map/reduce_scatter | solution.py:171
  138.0 3.1 %copy-start.6 = (bf16[4,256,10,64]{1,0,3,2:T(4,128)(2,1)S(1)}, bf16[4,256,10,64]{1,0,3,2:T(4,128)(2,1)}, u32[]{:S(2)}) copy-start(bf16[4,256,10,64]{1,0,3,2:T(4,128)(2,1)} %reshape.400) | copy-start | bytes 3932164
  138.0 3.1 %copy-start.9 = (f32[4,256,256]{2,1,0:T(8,128)S(1)}, f32[4,256,256]{2,1,0:T(8,128)}, u32[]{:S(2)}) copy-start(f32[4,256,256]{2,1,0:T(8,128)} %fusion.78) | copy-start | bytes 3145732
  138.0 3.1 %copy-start.18 = (f32[4,10,256]{2,1,0:T(8,128)S(1)}, f32[4,10,256]{2,1,0:T(8,128)}, u32[]{:S(2)}) copy-start(f32[4,10,256]{2,1,0:T(8,128)} %copy.63) | copy-start | bytes 122884
  138.0 3.1 %copy-start.22 = (f32[4,256,10]{1,2,0:T(8,128)S(1)}, f32[4,256,10]{1,2,0:T(8,128)}, u32[]{:S(2)}) copy-start(f32[4,256,10]{1,2,0:T(8,128)} %copy.72) | copy-start | bytes 122884
  139.3 5.9 %copy-start.15 = (pred[4,256,256]{2,1,0:T(8,128)(4,1)}, pred[4,256,256]{2,1,0:T(8,128)(4,1)S(1)}, u32[]{:S(2)}) copy-start(pred[4,256,256]{2,1,0:T(8,128)(4,1)S(1)} %compare_and_fusion) | copy-start | bytes 786436
  161.1 19.3 %copy-start.26 = (f32[10]{0:T(128)S(1)}, f32[10]{0:T(128)}, u32[]{:S(2)}) copy-start(f32[10]{0:T(128)} %copy-done.25) | copy-start | bytes 124
  161.1 20.6 %copy-start.12 = (bf16[1024,128]{1,0:T(8,128)(2,1)S(1)}, bf16[1024,128]{1,0:T(8,128)(2,1)}, u32[]{:S(2)}) copy-start(bf16[1024,128]{1,0:T(8,128)(2,1)} %param.11) | copy-start | bytes 786436
  177.5 2.8 %copy-start.5 = (f32[1,10,64,128]{3,2,1,0:T(8,128)S(1)}, f32[1,10,64,128]{3,2,1,0:T(8,128)}, u32[]{:S(2)}) copy-start(f32[1,10,64,128]{3,2,1,0:T(8,128)} %get-tuple-element.59) | copy-start | bytes 983044
  180.2 1.9 copy-start.7
  180.2 1.9 copy-start.10
  180.3 1.9 copy-start.16
  (10 other events, 13.5 us)
Sparse Core Ops, SparseCore 0:
  69.2 41.3 all-gather.5
  137.9 39.5 all-gather.7
  180.6 41.1 reduce-scatter.1
